TPU v7x, 256 devices: a whole 4x4x8 slice. The times are simulated.
256 devices in a mesh: depth: 32 (over y, x, core), rows: 8 (over z).
Axes of the slice: x: 4, y: 4, z: 8, core: 2. Of those that a mesh axis runs over, the one named last changes fastest.
Arguments:
- initial: float32 [32, 256, 128], P('rows'), may hold values from -6 to 6
- forward_guess: float32 [64, 32, 256, 128], P('depth', 'rows'), may hold values from -6 to 6
- adjoint_guess: float32 [64, 32, 256, 128], P('depth', 'rows'), may hold values from -6 to 6
- cotangent: float32 [32, 256, 128], P('rows'), may hold values from -6 to 6
- kernel: bfloat16 [3, 3, 128, 128], replicated, may hold values from -0.125 to 0.125
- conv_bias: float32 [128], replicated, may hold values from -1.5 to 1.5
Outputs:
- states: float32 [64, 32, 256, 128], P('depth', 'rows')
- adjoints: float32 [64, 32, 256, 128], P('depth', 'rows')
- grad_kernel: float32 [3, 3, 128, 128], replicated
- grad_bias: float32 [128], replicated
All inputs are finite; a program needn't handle non-finite values.
Results may differ from a plain program's by a relative error of at most 0.0025.
The roundings to bfloat16 on the way count: a program that leaves them out, or rounds other values in their place, can miss the bound.
Values may be sent and summed in bfloat16 or wider, within the bound.
No kernel may reach another device: no remote copies, remote signals or barrier semaphores. Data moves between devices by JAX's collectives and lax.ppermute only.
A program may use at most 64 MiB of HBM per device.

v0:
```python
import jax
import jax.numpy as jnp
from jax import lax
from jax.sharding import PartitionSpec as P

STEP_SIZE = 0.2


def padded_2(shard, sides, width):
    for axis, dim in sides:
        devices, length = (lax.axis_size(axis), shard.shape[dim])
        up = [(i, (i + 1) % devices) for i in range(devices - 1)]
        down = [(j, i) for i, j in up]
        last = lax.slice_in_dim(shard, length - width, length, axis=dim)
        leading = lax.slice_in_dim(shard, 0, width, axis=dim)
        before = lax.ppermute(last, axis, up)
        after = lax.ppermute(leading, axis, down)
        shard = jnp.concatenate([before, shard, after], axis=dim)
    return shard


def passed_along(value, axis, steps):
    count = lax.axis_size(axis)
    leading, last = (max(0, -steps), min(count, count - steps))
    return lax.ppermute(value, axis, [(source, source + steps) for source in range(leading, last)])


def restrict(signal):
    row_count, col_count, channels = signal.shape
    return signal.reshape(row_count // 2, 2, col_count // 2, 2, channels).mean(axis=(1, 3))


def prolong(signal):
    return jnp.repeat(jnp.repeat(signal, 2, axis=0), 2, axis=1)


def taps_product(padded, kernel, row_count, col_count):
    summed = jnp.zeros((row_count * col_count, kernel.shape[3]), jnp.float32)
    for row_tap in range(3):
        for col_tap in range(3):
            window = padded[row_tap : row_tap + row_count, col_tap : col_tap + col_count].reshape(
                row_count * col_count, -1
            )
            summed = summed + jnp.dot(
                window, kernel[row_tap, col_tap], preferred_element_type=jnp.float32
            )
    return summed.reshape(row_count, col_count, -1)


def surround(signal, on_coarse):
    if on_coarse:
        padded = padded_2(signal, (("rows", 0),), 1)
    else:
        padded = padded_2(signal, (("rows", 0),), 1)
    return jnp.pad(padded, ((0, 0), (1, 1), (0, 0)))


def advance(current, kernel, conv_bias, on_coarse):
    factor = 2.0 * STEP_SIZE if on_coarse else STEP_SIZE
    squashed = jnp.tanh(current).astype(jnp.bfloat16)
    padded = surround(squashed, on_coarse)
    return current + factor * (
        taps_product(padded, kernel, current.shape[0], current.shape[1]) + conv_bias
    )


def retreat(current, adjoint, kernel_flip, on_coarse):
    factor = 2.0 * STEP_SIZE if on_coarse else STEP_SIZE
    derivative = 1.0 - jnp.tanh(current) ** 2
    padded = surround(adjoint.astype(jnp.bfloat16), on_coarse)
    return adjoint + factor * derivative * taps_product(
        padded, kernel_flip, adjoint.shape[0], adjoint.shape[1]
    )


def kernel_terms(padded, cotan, row_count, col_count):
    flat = cotan.reshape(row_count * col_count, -1)
    tap_rows = []
    for row_tap in range(3):
        tap_cols = []
        for col_tap in range(3):
            window = padded[row_tap : row_tap + row_count, col_tap : col_tap + col_count].reshape(
                row_count * col_count, -1
            )
            tap_cols.append(
                lax.dot_general(
                    window, flat, (((0,), (0,)), ((), ())), preferred_element_type=jnp.float32
                )
            )
        tap_rows.append(jnp.stack(tap_cols))
    return jnp.stack(tap_rows)


def shards(initial, forward_guess, adjoint_guess, cotangent, kernel, conv_bias):
    block_count = lax.axis_size("depth")
    depth_pos = lax.axis_index("depth")
    at_first = depth_pos == 0
    at_last = depth_pos == block_count - 1
    row_count, col_count = (initial.shape[0], initial.shape[1])
    kernel_flip = jnp.transpose(jnp.flip(kernel, (0, 1)), (0, 1, 3, 2))
    coarse_start = restrict(initial)
    guess_point = forward_guess[1]
    previous = passed_along(guess_point, "depth", 1)
    previous = jnp.where(at_first, initial, previous)
    relaxed_odd = advance(previous, kernel, conv_bias, False)
    rhs_local = restrict(advance(relaxed_odd, kernel, conv_bias, False)) - advance(
        restrict(previous), kernel, conv_bias, True
    )

    def forward_turn(step_no, state_pair):
        incoming, kept_state = state_pair
        result = advance(incoming, kernel, conv_bias, True) + rhs_local
        kept_state = jnp.where(step_no == depth_pos, result, kept_state)
        incoming = passed_along(result, "depth", 1)
        return (incoming, kept_state)

    last_coarse, stored = lax.fori_loop(
        0, block_count, forward_turn, (coarse_start, jnp.zeros_like(coarse_start))
    )
    corrected = guess_point + prolong(stored - restrict(guess_point))
    prev_fixed, prev_coarse = passed_along((corrected, stored), "depth", 1)
    prev_fixed = jnp.where(at_first, initial, prev_fixed)
    linear = jnp.where(at_first, coarse_start, prev_coarse)
    state_odd = advance(prev_fixed, kernel, conv_bias, False)
    guess_even = adjoint_guess[0]
    ahead = passed_along(guess_even, "depth", -1)
    ahead = jnp.where(at_last, cotangent, ahead)
    relaxed_adj = retreat(state_odd, ahead, kernel_flip, False)
    residual = retreat(prev_fixed, relaxed_adj, kernel_flip, False) - guess_even
    coarse_res = restrict(residual)

    def backward_turn(step_no, state_pair):
        incoming, kept_error = state_pair
        result = retreat(linear, incoming, kernel_flip, True) + coarse_res
        kept_error = jnp.where(step_no == block_count - 1 - depth_pos, result, kept_error)
        incoming = passed_along(result, "depth", -1)
        return (incoming, kept_error)

    final_error, error_own = lax.fori_loop(
        0, block_count, backward_turn, (jnp.zeros_like(coarse_start), jnp.zeros_like(coarse_start))
    )
    corrected_adj = guess_even + prolong(error_own)
    ahead_fixed = passed_along(corrected_adj, "depth", -1)
    ahead_fixed = jnp.where(at_last, cotangent, ahead_fixed)
    adjoint_odd = retreat(state_odd, ahead_fixed, kernel_flip, False)
    squashed_even = surround(jnp.tanh(prev_fixed).astype(jnp.bfloat16), False)
    squashed_odd = surround(jnp.tanh(state_odd).astype(jnp.bfloat16), False)
    local_grad = kernel_terms(squashed_even, adjoint_odd.astype(jnp.bfloat16), row_count, col_count)
    local_grad = local_grad + kernel_terms(
        squashed_odd, ahead_fixed.astype(jnp.bfloat16), row_count, col_count
    )
    local_bias = jnp.sum(adjoint_odd, axis=(0, 1)) + jnp.sum(ahead_fixed, axis=(0, 1))
    grad_sum, bias_sum = lax.psum((local_grad, local_bias), ("depth", "rows"))
    factor = STEP_SIZE / (row_count * lax.axis_size("rows") * col_count)
    states_out = jnp.stack([state_odd, corrected])
    adjoints_out = jnp.stack([corrected_adj, adjoint_odd])
    return (states_out, adjoints_out, grad_sum * factor, bias_sum * factor)


def solution(mesh):
    placed = (
        P("rows", None, None),
        P("depth", "rows", None, None),
        P("depth", "rows", None, None),
        P("rows", None, None),
        P(),
        P(),
    )
    return jax.shard_map(
        shards,
        mesh=mesh,
        in_specs=placed,
        out_specs=(P("depth", "rows", None, None), P("depth", "rows", None, None), P(), P()),
        check_vma=False,
    )
```

profile of v0, /device:TPU:1, one launch (start us, length us, event | category | flops | bytes accessed | tf_op | source)
XLA Modules:
  0.0 1818.0 jit_solution(15526250043578704130)
XLA Ops:
  127.0 579.7 %while.36 = (s32[]{:T(128)}, f32[2,128,128]{2,1,0:T(8,128)S(1)}, f32[2,128,128]{2,1,0:T(8,128)S(1)}, bf16[3,3,128,128]{3,2,1,0:T(8,128)(2,1)S(1)}, f32[128]{0:T(...) while((s32[]{:T(128)}, f32[2,128,128]{2,1,0:T(8,128)S(1)}, ...), condition=%wide.region_4.5_spmd.clone, body=%wide.region_3.4_spmd.clone.sunk | while | flops 76853248 | bytes 6327017 | solution.py:117
  355.8 7.6 collective-permute-start.2
  374.8 7.6 collective-permute-start.2
  393.7 7.6 collective-permute-start.2
  412.7 7.6 collective-permute-start.2
  431.7 7.6 collective-permute-start.2
  450.6 7.6 collective-permute-start.2
  469.6 7.6 collective-permute-start.2
  488.5 7.6 collective-permute-start.2
  507.5 7.6 collective-permute-start.2
  526.5 7.6 collective-permute-start.2
  545.4 7.6 collective-permute-start.2
  564.4 7.6 collective-permute-start.2
  583.4 7.6 collective-permute-start.2
  602.3 7.6 collective-permute-start.2
  621.3 7.6 collective-permute-start.2
  640.3 7.6 collective-permute-start.2
  678.2 7.6 collective-permute-start.2
  810.8 659.7 %while.37 = (s32[]{:T(128)}, f32[2,128,128]{2,1,0:T(8,128)S(1)}, f32[2,128,128]{2,1,0:T(8,128)S(1)}, f32[2,128,128]{2,1,0:T(8,128)S(1)}, bf16[3,3,128,128]{3,2,1...) while((s32[]{:T(128)}, f32[2,128,128]{2,1,0:T(8,128)S(1)}, ...), condition=%wide.region_8.9_spmd.clone, body=%wide.region_7.8_spmd.clone.sunk | while | flops 76886016 | bytes 7244093 | solution.py:139
  824.9 10.2 collective-permute-done.5
  868.0 10.2 collective-permute-done.5
  911.1 10.8 collective-permute-done.5
  1531.3 105.2 %psum.15 = f32[128]{0:T(128)S(1)} all-reduce(f32[128]{0:T(128)S(1)} %add.599), channel_id=1, replica_groups=mesh['depth'=32,'rows'=8] {'depth','rows'}, use_global_device_ids=true, to_apply=%region_12.13 | all-reduce | flops 128 | bytes 1024 | tf_op jit(solution)/shard_map/psum | solution.py:153
  1637.0 172.2 %all-reduce.12.cloned.1.call-done = f32[3,3,128,128]{3,2,1,0:T(8,128)} async-done(((f32[3,3,128,128]{3,2,1,0:T(8,128)}), f32[3,3,128,128]{3,2,1,0:T(8,128)}) %all-reduce.12.cloned.1.call-update) | async-done | bytes 589840 | tf_op jit(solution)/shard_map/psum | solution.py:153
  (1960 shorter events, 1355.9 us)
Async XLA Ops:
  7.2 1802.1 %all-reduce.12.cloned.1.call-start = ((), (), s32[]{:S(2)}) async-start(), calls=%async_computation | async-start | bytes 1179648 | tf_op jit(solution)/shard_map/psum | solution.py:153
  8.4 13.3 collective-permute-start.17
  27.8 16.5 collective-permute-start.11
  31.3 14.3 collective-permute-start.12
  35.0 14.3 collective-permute-start.18
  39.0 10.3 collective-permute-start.19
  40.3 19.8 %collective-permute-start.7 = (bf16[1,256,128]{1,2,0:T(8,128)(2,1)}, bf16[1,256,128]{1,2,0:T(8,128)(2,1)S(1)}, u32[]{:S(2)}, u32[]{:S(2)}) collective-permute-start(bf16[1,256,128]{1,2,0:T(8,128)(2,1)} %get-tuple-element.543), channel_id=1, source_target_pairs={{0,1},{1,2},{2,3},{3,4},{4,5},{5,6},{6,7},{8,9},{9,10},{10,11},{11... | collective-permute-start | bytes 196616 | tf_op jit(solution)/shard_map/ppermute | solution.py:16
  44.3 15.8 collective-permute-start.8
  85.2 13.3 collective-permute-start.10
  86.5 12.0 collective-permute-start.9
  355.8 9.5 collective-permute-start.2
  393.7 9.5 collective-permute-start.2
  412.7 9.5 collective-permute-start.2
  708.0 13.0 collective-permute-start.13
  723.7 16.0 collective-permute-start.14
  728.8 10.8 collective-permute-start.15
  731.3 42.4 %collective-permute-start.16 = (f32[2,128,128]{2,1,0:T(8,128)S(1)}, f32[2,128,128]{2,1,0:T(8,128)}, u32[]{:S(2)}, u32[]{:S(2)}) collective-permute-start(f32[2,128,128]{2,1,0:T(8,128)S(1)} %get-tuple-element.361), channel_id=1, source_target_pairs={{0,8},{8,16},{16,24},{24,32},{32,40},{40,48},{48,56},{56,64},{64,7... | collective-permute-start | bytes 393224 | tf_op jit(solution)/shard_map/ppermute | solution.py:25
  765.8 9.7 collective-permute-start.20
  823.0 12.2 collective-permute-start.5
  866.0 12.1 collective-permute-start.5
  909.1 12.7 collective-permute-start.5
  1475.5 18.2 %collective-permute-start.22 = (f32[4,256,128]{1,2,0:T(8,128)}, f32[4,256,128]{1,2,0:T(8,128)}, u32[]{:S(2)}, u32[]{:S(2)}) collective-permute-start(f32[4,256,128]{1,2,0:T(8,128)} %bitcast_add_fusion), channel_id=1, source_target_pairs={{8,0},{16,8},{24,16},{32,24},{40,32},{48,40},{56,48},{64,56},{72,6... | collective-permute-start | bytes 1572872 | tf_op jit(solution)/shard_map/ppermute | solution.py:25
  1480.7 12.7 collective-permute-start.25
  1498.4 9.9 collective-permute-start.23
  (370 other events, 2269.7 us)
Sparse Core Ops, SparseCore 0:
  1529.7 279.5 all-reduce.11
where the time goes:
time: 1830 us; the launch traced here: 1820 us
  starting transfers between devices  785 us (43%)
  waiting for transfers between devices  524 us (29%)
  local copies, waits for them, and re-layouts  184 us (10%)
  matrix products  117 us (6%)
  blocking collectives  105 us (6%)
  other arithmetic  78.5 us (4%)
    ppermute x72, starting transfers between devices, padded_2(): before = lax.ppermute(last, axis, up)  393 us
    ppermute x69, starting transfers between devices, passed_along(): lax.ppermute(value, axis, [(source, source + steps) for source in range(l...  299 us
    ppermute x69, waiting for transfers between devices, passed_along(): lax.ppermute(value, axis, [(source, source + steps) for source in range(l...  283 us
    psum x1, waiting for transfers between devices, shards(): grad_sum, bias_sum = lax.psum((local_grad, local_bias), ('depth', 'rows'))  172 us
    dot_general x639, matrix products, taps_product(): jnp.dot(window, kernel[row_tap, col_tap], preferred_element_type=jnp.floa...  113 us
    psum x1, blocking collectives, shards(): grad_sum, bias_sum = lax.psum((local_grad, local_bias), ('depth', 'rows'))  105 us
    ppermute x72, starting transfers between devices, padded_2(): after = lax.ppermute(leading, axis, down)  93.1 us
    slice x119, local copies, waits for them, and re-layouts, taps_product(): padded[row_tap:row_tap + row_count, col_tap:col_tap + col_count]  79.3 us
  transfers between devices with their start and end apart: 214, of which 132 were waited for; matrix products, arithmetic and copies ran while one was open for 4% of the time, Pallas kernels for 0%

commit v1 on v0

--- a/solution.py
+++ b/solution.py
@@ -150,7 +150,7 @@
         squashed_odd, ahead_fixed.astype(jnp.bfloat16), row_count, col_count
     )
     local_bias = jnp.sum(adjoint_odd, axis=(0, 1)) + jnp.sum(ahead_fixed, axis=(0, 1))
-    grad_sum, bias_sum = lax.psum((local_grad, local_bias), ("depth", "rows"))
+    grad_sum, bias_sum = lax.psum(lax.psum((local_grad, local_bias), "rows"), "depth")
     factor = STEP_SIZE / (row_count * lax.axis_size("rows") * col_count)
     states_out = jnp.stack([state_odd, corrected])
     adjoints_out = jnp.stack([corrected_adj, adjoint_odd])

time: 1830 us -> 1670 us (0.913)
  local copies, waits for them, and re-layouts: 184 us -> 125 us
  waiting for transfers between devices: 524 us -> 473 us
  other arithmetic: 78.5 us -> 55.6 us
  blocking collectives: 105 us -> 83.6 us
    psum x1 -> x2, waiting for transfers between devices: 172 us -> 120 us  [the longest x1 86.2 us: shards(): lax.psum((local_grad, local_bias), 'rows')]
    while x192 -> x0, local copies, waits for them, and re-layouts: 36.7 us -> none
    psum x1 -> x2, blocking collectives: 105 us -> 83.6 us  [the longest x1 71.1 us: shards(): lax.psum(lax.psum((local_grad, local_bias), 'rows'), 'depth')]
    select_n x32, other arithmetic: 23.5 us -> 3.13 us  [backward_turn(): jnp.where(step_no == block_count - 1 - depth_pos, result, kept_error)]
    slice x72, local copies, waits for them, and re-layouts: 24.1 us -> 4.45 us  [padded_2(): last = lax.slice_in_dim(shard, length - width, length, axis=dim)]
  transfers between devices with their start and end apart: 214 -> 215, of which waited for: 132 -> 134; matrix products, arithmetic and copies ran while one was open for 4% -> 4% of each run, Pallas kernels for 0% -> 0%
where the time goes in v1:
time: 1670 us; the launch traced here: 1660 us
  starting transfers between devices  784 us (47%)
  waiting for transfers between devices  473 us (28%)
  local copies, waits for them, and re-layouts  125 us (7%)
  matrix products  117 us (7%)
  blocking collectives  83.6 us (5%)
  other arithmetic  55.6 us (3%)
    ppermute x72, starting transfers between devices, padded_2(): before = lax.ppermute(last, axis, up)  393 us
    ppermute x69, starting transfers between devices, passed_along(): lax.ppermute(value, axis, [(source, source + steps) for source in range(l...  298 us
    ppermute x69, waiting for transfers between devices, passed_along(): lax.ppermute(value, axis, [(source, source + steps) for source in range(l...  278 us
    dot_general x639, matrix products, taps_product(): jnp.dot(window, kernel[row_tap, col_tap], preferred_element_type=jnp.floa...  112 us
    ppermute x72, starting transfers between devices, padded_2(): after = lax.ppermute(leading, axis, down)  93.2 us
    psum x1, waiting for transfers between devices, shards(): lax.psum((local_grad, local_bias), 'rows')  86.2 us
    slice x119, local copies, waits for them, and re-layouts, taps_product(): padded[row_tap:row_tap + row_count, col_tap:col_tap + col_count]  79.3 us
    psum x1, blocking collectives, shards(): lax.psum(lax.psum((local_grad, local_bias), 'rows'), 'depth')  71.1 us
  transfers between devices with their start and end apart: 215, of which 134 were waited for; matrix products, arithmetic and copies ran while one was open for 4% of the time, Pallas kernels for 0%

profile of v1, /device:TPU:1, one launch (start us, length us, event | category | flops | bytes accessed | tf_op | source)
XLA Modules:
  0.0 1662.5 jit_solution(18264620251514977755)
XLA Ops:
  128.3 579.6 %while.36 = (s32[]{:T(128)}, f32[2,128,128]{2,1,0:T(8,128)S(1)}, f32[2,128,128]{2,1,0:T(8,128)S(1)}, bf16[3,3,128,128]{3,2,1,0:T(8,128)(2,1)S(1)}, f32[128]{0:T(...) while((s32[]{:T(128)}, f32[2,128,128]{2,1,0:T(8,128)S(1)}, ...), condition=%wide.region_4.5_spmd.clone, body=%wide.region_3.4_spmd.clone.sunk | while | flops 76853248 | bytes 6327017 | solution.py:117
  357.1 7.6 collective-permute-start.2
  376.0 7.6 collective-permute-start.2
  395.0 7.6 collective-permute-start.2
  414.0 7.6 collective-permute-start.2
  432.9 7.6 collective-permute-start.2
  451.9 7.6 collective-permute-start.2
  470.8 7.6 collective-permute-start.2
  489.8 7.6 collective-permute-start.2
  508.8 7.6 collective-permute-start.2
  527.7 7.6 collective-permute-start.2
  546.7 7.6 collective-permute-start.2
  565.7 7.6 collective-permute-start.2
  584.6 7.6 collective-permute-start.2
  641.5 7.6 collective-permute-start.2
  679.5 7.6 collective-permute-start.2
  810.0 578.3 %while.37 = (s32[]{:T(128)}, f32[2,128,128]{2,1,0:T(8,128)S(1)}, f32[2,128,128]{2,1,0:T(8,128)S(1)}, f32[2,128,128]{2,1,0:T(8,128)S(1)}, bf16[3,3,128,128]{3,2,1...) while((s32[]{:T(128)}, f32[2,128,128]{2,1,0:T(8,128)S(1)}, ...), condition=%wide.region_8.9_spmd.clone, body=%wide.region_7.8_spmd.clone.sunk | while | flops 76886016 | bytes 6457577 | solution.py:139
  821.7 11.0 collective-permute-done.5
  859.6 11.0 collective-permute-done.5
  898.0 11.2 collective-permute-done.5
  1447.9 86.2 %all-reduce.13.cloned.1.call-done = f32[3,3,128,128]{3,2,1,0:T(8,128)} async-done(((f32[3,3,128,128]{3,2,1,0:T(8,128)}), f32[3,3,128,128]{3,2,1,0:T(8,128)}) %all-reduce.13.cloned.1.call-update) | async-done | bytes 589840 | tf_op jit(solution)/shard_map/psum | solution.py:153
  1535.6 12.5 psum.30
  1548.1 71.1 %psum.31 = f32[128]{0:T(128)S(1)} all-reduce(f32[128]{0:T(128)S(1)} %psum.30), channel_id=1, replica_groups=mesh['depth'=32,'rows'=8] {'depth'}, use_global_device_ids=true, to_apply=%region_14.15 | all-reduce | flops 128 | bytes 1024 | tf_op jit(solution)/shard_map/psum | solution.py:153
  1619.7 34.0 %all-reduce.15.cloned.1.call-done = f32[3,3,128,128]{3,2,1,0:T(8,128)} async-done(((f32[3,3,128,128]{3,2,1,0:T(8,128)}), f32[3,3,128,128]{3,2,1,0:T(8,128)}) %all-reduce.15.cloned.1.call-update) | async-done | bytes 589840 | tf_op jit(solution)/shard_map/psum | solution.py:153
  (1772 shorter events, 1287.8 us)
Async XLA Ops:
  7.2 1527.0 %all-reduce.13.cloned.1.call-start = ((), (), s32[]{:S(2)}) async-start(), calls=%async_computation | async-start | bytes 1179648 | tf_op jit(solution)/shard_map/psum | solution.py:153
  8.4 13.3 collective-permute-start.17
  27.8 16.5 collective-permute-start.11
  31.3 14.2 collective-permute-start.12
  35.0 14.3 collective-permute-start.18
  39.0 10.3 collective-permute-start.19
  40.3 20.0 %collective-permute-start.7 = (bf16[1,256,128]{1,2,0:T(8,128)(2,1)}, bf16[1,256,128]{1,2,0:T(8,128)(2,1)S(1)}, u32[]{:S(2)}, u32[]{:S(2)}) collective-permute-start(bf16[1,256,128]{1,2,0:T(8,128)(2,1)} %get-tuple-element.543), channel_id=1, source_target_pairs={{0,1},{1,2},{2,3},{3,4},{4,5},{5,6},{6,7},{8,9},{9,10},{10,11},{11... | collective-permute-start | bytes 196616 | tf_op jit(solution)/shard_map/ppermute | solution.py:16
  44.3 16.0 collective-permute-start.8
  85.2 13.3 collective-permute-start.10
  86.5 12.0 collective-permute-start.9
  357.1 9.5 collective-permute-start.2
  395.0 9.5 collective-permute-start.2
  432.9 9.5 collective-permute-start.2
  470.8 9.5 collective-permute-start.2
  489.8 9.5 collective-permute-start.2
  709.3 13.0 collective-permute-start.13
  724.2 15.6 collective-permute-start.14
  730.0 9.8 collective-permute-start.15
  732.5 42.2 %collective-permute-start.16 = (f32[2,128,128]{2,1,0:T(8,128)S(1)}, f32[2,128,128]{2,1,0:T(8,128)}, u32[]{:S(2)}, u32[]{:S(2)}) collective-permute-start(f32[2,128,128]{2,1,0:T(8,128)S(1)} %get-tuple-element.361), channel_id=1, source_target_pairs={{0,8},{8,16},{16,24},{24,32},{32,40},{40,48},{48,56},{56,64},{64,7... | collective-permute-start | bytes 393224 | tf_op jit(solution)/shard_map/ppermute | solution.py:25
  819.8 12.9 collective-permute-start.5
  857.7 12.9 collective-permute-start.5
  896.0 13.1 collective-permute-start.5
  1390.7 14.2 collective-permute-start.22
  1441.6 212.2 %all-reduce.15.cloned.1.call-start = ((), (), s32[]{:S(2)}) async-start(), calls=%async_computation.1 | async-start | bytes 1179648 | tf_op jit(solution)/shard_map/psum | solution.py:153
  (275 other events, 2879.5 us)
Sparse Core Ops, SparseCore 0:
  1441.7 92.4 all-reduce.12
  1537.4 116.2 all-reduce.14
